TPU v7x, 256 devices: a whole 4x4x8 slice. The times are simulated.
256 devices in a mesh: space: 32 (over x_lo, z, core), src: 8 (over y, x_hi).
Axes of the slice: x: 4 (x_hi: 2, x_lo: 2; x = x_hi * 2 + x_lo), y: 4, z: 8, core: 2. Of those that a mesh axis runs over, the one named last changes fastest.
Arguments:
- medium: float32 [32, 64, 64, 64], P('space'), may hold values from 0.8 to 1.2
- source_cells: int32 [8, 4096], P('src'), may hold values from 0 to 8388607, as said below
- source_weights: float32 [2, 8, 4096], P(None, 'src'), may hold values from -48 to 48
- adjoint: bfloat16 [2, 8, 32, 64, 64, 64], P(None, 'src', 'space'), may hold values from -6 to 6
Outputs:
- field: float32 [2, 8, 32, 64, 64, 64], P(None, 'src', 'space')
- gradient: float32 [32, 64, 64, 64], P('space', 'src')
Inputs may be any that keep to these rules, and one draw needn't show every extreme that they name: source_cells[s, p] is the cell b * 64**3 + (x * 64 + y) * 64 + z of the point p of source s; points may repeat and fall in any box.
All inputs are finite; a program needn't handle non-finite values.
Results may differ from a plain program's by a relative error of at most 0.0003.
Values sent between devices are 32-bit elements; how exact they have to be, the bound alone decides.
A program may use at most 128 MiB of HBM per device.

v0:
```python
import functools

import jax
import jax.numpy as jnp
import numpy as np
from jax import lax
from jax.experimental import pallas as pl
from jax.experimental.pallas import tpu as pltpu
from jax.sharding import PartitionSpec as P

N = 64
ROWS = N * N
LANES = 2 * N
TERMS = 2
BGX, BGY, BGZ = 2, 4, 4
SRC = 8
SLAB = N // SRC
CH = SLAB * N
DAMP = 0.25
PITCH = 72
BACK, BACKS = 512, 4
ITEM = 2048
MESH = pl.DeviceIdType.MESH
SLOTS = 256
F32, BF16 = jnp.float32, jnp.bfloat16


def split(values):
    high = values.astype(BF16)
    low = (values - high.astype(F32)).astype(BF16)
    return high, low


def dft_table(sign):
    k = np.arange(N)
    phase = 2.0 * np.pi / N * (k[:, None] * k[None, :] % N)
    c, s = np.cos(phase), sign * np.sin(phase)
    w = np.block([[c, s], [-s, c]]).astype(np.float32)
    high = w.astype(BF16)
    low = (w - high.astype(np.float32)).astype(BF16)
    half = np.concatenate([high, low], axis=1)
    return np.concatenate([half, half], axis=0)


def along_lanes(values, table):
    high, low = split(values)
    out = jnp.dot(jnp.concatenate([high, low], axis=1), table, preferred_element_type=F32)
    return out[:, :LANES] + out[:, LANES:]


def lower_half(rows):
    return lax.broadcasted_iota(jnp.int32, (rows, LANES), 1) < N


def trade(first, second):
    lower = lower_half(first.shape[0])
    crossed = pltpu.roll(jnp.where(lower, second, first), N, 1)
    return jnp.where(lower, first, crossed), jnp.where(lower, crossed, second)


def product_swapped(values, table, exchange=False):
    blocks = []
    for start in range(0, values.shape[0], 2 * LANES):
        high, low = split(values[start : start + 2 * LANES])
        both = jnp.concatenate([high, low], axis=1)
        out = lax.dot_general(table, both, (((1,), (1,)), ((), ())), preferred_element_type=F32)
        out = out[:LANES] + out[LANES:]
        for pair in range(out.shape[1] // LANES):
            turned = out[:, pair * LANES : (pair + 1) * LANES]
            first, second = turned[:N], turned[N:]
            blocks += trade(second, first) if exchange else trade(first, second)
    return jnp.concatenate(blocks, axis=0)


def staggered(count, stages):
    held = {}
    for turn in range(count + len(stages) - 1):
        for n in reversed(range(len(stages))):
            item = turn - n
            if 0 <= item < count:
                held[item] = stages[n](item, held.get(item))


def place_kernel(box_ref, cells_ref, weights_ref, out_ref, pos_ref, feat_ref):
    cells = cells_ref[...] - box_ref[0] * (N * N * N)
    inside = (cells >= 0) & (cells < N * N * N)
    mask = jnp.where(inside, 1.0, 0.0).astype(BF16)
    groups = cells.shape[0]
    i0 = lax.broadcasted_iota(jnp.int32, (128, 128), 0)
    i1 = lax.broadcasted_iota(jnp.int32, (128, 128), 1)
    upper = jnp.where(i0 < i1, 1.0, 0.0).astype(BF16)
    within = jnp.dot(mask, upper, preferred_element_type=F32)
    totals = jnp.dot(mask, jnp.ones((128, 128), BF16), preferred_element_type=F32)
    j0 = lax.broadcasted_iota(jnp.int32, (groups, groups), 0)
    j1 = lax.broadcasted_iota(jnp.int32, (groups, groups), 1)
    before = jnp.where(j1 < j0, 1.0, 0.0).astype(BF16)
    offset = jnp.dot(before, totals.astype(BF16), preferred_element_type=F32)
    pos_ref[...] = jnp.where(inside, (within + offset).astype(jnp.int32), -1)
    count = jnp.sum(jnp.where(inside, 1, 0))
    safe = jnp.where(inside, cells, 0)
    rh, rl = split(weights_ref[0])
    ih, il = split(weights_ref[1])
    rows = (
        (safe >> 13).astype(F32),
        ((safe >> 6) & (N - 1)).astype(F32),
        (((safe >> 12) & 1) * N + (safe & (N - 1))).astype(F32),
        rh.astype(F32),
        rl.astype(F32),
        ih.astype(F32),
        il.astype(F32),
    )
    for n, row in enumerate(rows):
        feat_ref[n] = row

    def chunk(step, carry):
        slot = lax.broadcasted_iota(jnp.int32, (SLOTS, 128), 0) + step * SLOTS
        sub = lax.broadcasted_iota(jnp.int32, (16, 128), 0)
        hots, feats = [], []
        for g in range(groups):
            hots.append(jnp.where(pos_ref[g : g + 1, :] == slot, 1.0, 0.0).astype(BF16))
            f = jnp.zeros((16, 128), F32)
            for n in range(len(rows)):
                f = jnp.where(sub == n, feat_ref[n, g : g + 1, :], f)
            feats.append(f.astype(BF16))
        hot = jnp.concatenate(hots, axis=1)
        feat = jnp.concatenate(feats, axis=1)
        nt = (((1,), (1,)), ((), ()))
        by_lane = lax.dot_general(feat, hot, nt, preferred_element_type=F32)
        by_row = by_lane.T
        used = lax.broadcasted_iota(jnp.int32, (1, SLOTS), 1) + step * SLOTS < count
        plane = (by_lane[0:1] * N + by_lane[1:2]).astype(jnp.int32)
        plane = jnp.where(used, plane, -1)
        lane = lax.broadcasted_iota(jnp.int32, (SLOTS, LANES), 1)
        hit = lane == by_row[:, 2:3].astype(jnp.int32)
        spread = [jnp.where(hit, by_row[:, n : n + 1], 0.0) for n in range(3, 7)]
        spread = jnp.concatenate(spread, axis=1).astype(BF16)

        def rows_of(block, inner):
            start = pl.multiple_of(block * 256, 256)
            at = lax.broadcasted_iota(jnp.int32, (256, SLOTS), 0) + start
            pick = jnp.where(at == plane, 1.0, 0.0).astype(BF16)
            got = jnp.dot(pick, spread, preferred_element_type=F32)
            for part in range(2):
                one = got[:, 2 * part * LANES : (2 * part + 1) * LANES]
                one = one + got[:, (2 * part + 1) * LANES : (2 * part + 2) * LANES]
                old = out_ref[part, pl.ds(start, 256), :]
                out_ref[part, pl.ds(start, 256), :] = jnp.where(step > 0, old, 0.0) + one
            return inner

        return lax.fori_loop(0, ROWS // 512, rows_of, carry)

    lax.fori_loop(0, jnp.maximum(1, (count + SLOTS - 1) // SLOTS), chunk, 0)


def place(box, cells, weights):
    groups = cells.shape[-1] // 128
    return pl.pallas_call(
        place_kernel,
        out_shape=jax.ShapeDtypeStruct((2, ROWS // 2, LANES), F32),
        in_specs=[pl.BlockSpec(memory_space=pltpu.SMEM)]
        + [pl.BlockSpec(memory_space=pltpu.VMEM)] * 2,
        out_specs=pl.BlockSpec(memory_space=pltpu.VMEM),
        scratch_shapes=[pltpu.VMEM((groups, 128), jnp.int32), pltpu.VMEM((8, groups, 128), F32)],
        compiler_params=pltpu.CompilerParams(vmem_limit_bytes=12 * 1024 * 1024),
    )(box, cells.reshape(groups, 128), weights.reshape(2, groups, 128))


def series_kernel(
    remote,
    eig_ref, source_ref, medium_hbm, pair_hbm, wave_hbm, fwd_hbm, inv_hbm, turn_hbm, adjoint_hbm,
    out_hbm, grad_ref,
    packed, drive, one, two, kre, kim, pot, medium, pair_ref, wave_ref, fwd_ref, inv_ref, turn_ref, adjoint,
    faces, ratios, ends, turns, sums, zcor, recv, gsend, grecv,
    send_sem, recv_sem, gsend_sem, grecv_sem, out_sem, in_sem,
):
    fre, fim = packed.at[0], packed.at[1]
    loads = [
        pltpu.make_async_copy(there, here, in_sem.at[n])
        for n, (there, here) in enumerate(
            (
                (pair_hbm, pair_ref),
                (medium_hbm, medium),
                (wave_hbm, wave_ref),
                (fwd_hbm, fwd_ref),
                (inv_hbm, inv_ref),
                (turn_hbm, turn_ref),
                (adjoint_hbm, adjoint),
            )
        )
    ]
    for load in loads:
        load.start()
    if remote:
        space, me = lax.axis_index("space"), lax.axis_index("src")
        bx, by, bz = space // (BGY * BGZ), space // BGZ % BGY, space % BGZ
        below = (
            lax.rem(bx + BGX - 1, BGX) * (BGY * BGZ) + by * BGZ + bz,
            bx * (BGY * BGZ) + lax.rem(by + BGY - 1, BGY) * BGZ + bz,
            bx * (BGY * BGZ) + by * BGZ + lax.rem(bz + BGZ - 1, BGZ),
        )
        above = (
            lax.rem(bx + 1, BGX) * (BGY * BGZ) + by * BGZ + bz,
            bx * (BGY * BGZ) + lax.rem(by + 1, BGY) * BGZ + bz,
            bx * (BGY * BGZ) + by * BGZ + lax.rem(bz + 1, BGZ),
        )
        has_below = [(v > 0).astype(F32) for v in (bx, by, bz)]
        has_above = [(v < e - 1).astype(F32) for v, e in ((bx, BGX), (by, BGY), (bz, BGZ))]
        barrier = pltpu.get_barrier_semaphore()
        for d in range(3):
            for other in (below[d], above[d]):
                pl.semaphore_signal(barrier, 1, device_id={"space": other}, device_id_type=MESH)
        for k in range(1, SRC):
            pl.semaphore_signal(
                barrier, 1, device_id={"src": lax.rem(me + k, SRC)}, device_id_type=MESH
            )
    else:
        me = 0

    low = lower_half(N)

    def table(z, carry):
        rows = pl.ds(pl.multiple_of(z * N, N), N)
        shifted = pair_ref[...] + eig_ref[z]
        scale = 1.0 / ((shifted * shifted + DAMP * DAMP) * float(N**3))
        kre[rows, :] = shifted * scale
        kim[rows, :] = jnp.where(low, -DAMP, DAMP) * scale
        return carry

    loads[0].wait()
    lax.fori_loop(0, N, table, 0)

    def half_rows(pair):
        return pl.ds(pl.multiple_of(pair * N, N), N)

    def plane_rows(pair, half):
        return pl.ds(pl.multiple_of((2 * pair + half) * N, N), N)

    def pitched(pair, half):
        return pl.ds(pl.multiple_of((2 * pair + half) * PITCH, 8), N)

    def put_drive(pair, re, im):
        for half, rows in enumerate(trade(re, im)):
            drive[plane_rows(pair, half), :] = rows

    def begin(pair, carry):
        rows = half_rows(pair)
        fre[rows, :] = jnp.zeros((N, LANES), F32)
        fim[rows, :] = jnp.zeros((N, LANES), F32)
        put_drive(pair, source_ref[0, rows, :], source_ref[1, rows, :])
        return carry

    lax.fori_loop(0, N // 2, begin, 0)
    faces[...] = jnp.zeros_like(faces)
    zcor[...] = jnp.zeros_like(zcor)
    lane = lax.broadcasted_iota(jnp.int32, (N, LANES), 1)

    loads[1].wait()

    def potential(pair, carry):
        both = [medium[plane_rows(pair, half), :] - 1.0 for half in range(2)]
        both = jnp.concatenate(both, axis=1)
        pot[half_rows(pair), :] = both
        moved = pltpu.roll(both, 1 + 2 * pair, 1)
        ends[...] = jnp.where((lane % N) // 2 == pair, moved, ends[...])
        return carry

    lax.fori_loop(0, N // 2, potential, 0)
    turns[...] = jnp.concatenate([ends[...], ends[...]], axis=0).T
    half = N // 2
    for face, (even, odd) in enumerate(((1, N + 1), (N, 0))):
        ratios[2, face, pl.ds(0, half, stride=2), :] = turns[pl.ds(even, half, stride=2), :]
        ratios[2, face, pl.ds(1, half, stride=2), :] = turns[pl.ds(odd, half, stride=2), :]
    for d, planes in (
        (0, (pl.ds(0, N), pl.ds(ROWS - N, N))),
        (1, (pl.ds(0, N, stride=N), pl.ds(N - 1, N, stride=N))),
    ):
        for face in range(2):
            plane = medium[planes[face], :] - 1.0
            ratios[d, face] = jnp.concatenate([plane, plane], axis=1)
    ratios[...] = jnp.where(lower_half(N), -1.0 / DAMP, 1.0 / DAMP) * ratios[...]

    for load in loads[2:6]:
        load.wait()

    def forward():
        def load(p, _):
            return product_swapped(drive[pl.ds(p * ITEM, ITEM), :], turn_ref[...])

        def store(p, values):
            for n in range(ITEM // N):
                x = p * (ITEM // N) + n
                extra = (
                    zcor[0, pl.ds(x, 1), :]
                    + wave_ref[0] * zcor[1, pl.ds(x, 1), :]
                    + wave_ref[1] * zcor[2, pl.ds(x, 1), :]
                )
                to = pl.ds(x * PITCH, N)
                one[to, :] = values[n * N : (n + 1) * N] + extra

        staggered(ROWS // ITEM, (load, store))

    def middle():
        def strided(p, n):
            return pl.ds(p * (ITEM // N) + n, N, stride=PITCH)

        def load(p, _):
            values = [one[strided(p, n), :] for n in range(ITEM // N)]
            return product_swapped(jnp.concatenate(values, axis=0), turn_ref[...])

        def product(p, values):
            values = along_lanes(values, fwd_ref[...])
            rows = pl.ds(p * ITEM, ITEM)
            return kre[rows, :] * pltpu.roll(values, N, 1) - kim[rows, :] * values

        def store(p, values):
            values = product_swapped(values, turn_ref[...])
            for n in range(ITEM // N):
                two[strided(p, n), :] = values[n * N : (n + 1) * N]

        staggered(ROWS // ITEM, (load, product, store))

    def back_swap(item, ends):
        planes = []
        for n in range(BACK // N):
            x = item * (BACK // N) + n
            plane = two[pl.ds(pl.multiple_of(x * PITCH, 8), N), :]
            planes.append(plane)
            if ends:
                sums[0, pl.ds(x, 1), :] = jnp.sum(plane, axis=0, keepdims=True)
                for part in range(2):
                    waved = jnp.sum(wave_ref[part] * plane, axis=0, keepdims=True)
                    sums[1 + part, pl.ds(x, 1), :] = waved
        return product_swapped(jnp.concatenate(planes, axis=0), turn_ref[...], exchange=True)

    def back_rows(item):
        return pl.ds(pl.multiple_of(item * BACK, BACK), BACK)

    def updated(pair, even, odd):
        rows = half_rows(pair)
        gre, gim = trade(even, odd)
        ratio = pot[rows, :] * (1.0 / DAMP)
        return gre + ratio * (fim[rows, :] - gim), gim - ratio * (fre[rows, :] - gre)

    def finish_term(step):
        def swap_pass(i, inner):
            for p in range(BACKS):
                one[back_rows(i * BACKS + p), :] = back_swap(i * BACKS + p, True)
            return inner

        lax.fori_loop(0, ROWS // BACK // BACKS, swap_pass, 0)

        turned = lambda values: pltpu.roll(values, N, 1)
        edges = (
            (pl.ds(0, N), pl.ds(ROWS - N, N)),
            (pl.ds(0, N, stride=N), pl.ds(N - 1, N, stride=N)),
        )
        rows = [one[edges[d][face], :] for d in range(2) for face in range(2)]
        rows = along_lanes(jnp.concatenate(rows, axis=0), inv_ref[...])
        total = along_lanes(sums[...].reshape(3 * N, LANES), fwd_ref[...]).reshape(3, N, LANES)
        greens = (
            (rows[:N], rows[N : 2 * N]),
            (rows[2 * N : 3 * N], rows[3 * N :]),
            (turned(total[0]), turned(total[1]) + jnp.where(low, total[2], -total[2])),
        )
        if remote:

            @pl.when(step == 0)
            def _():
                pl.semaphore_wait(barrier, 6 + SRC - 1)

        copies = {}
        for d in (1, 2, 0):
            for face in range(2):
                green = greens[d][face]
                faces[d, face] = green - ratios[d, face] * turned(faces[d, face] - green)
            if remote:
                for side, other in ((1, above[d]), (0, below[d])):
                    slot = 1 - side
                    copies[d, slot] = pltpu.make_async_remote_copy(
                        src_ref=faces.at[d, side],
                        dst_ref=recv.at[step, 2 * d + slot],
                        send_sem=send_sem.at[step, 2 * d + slot],
                        recv_sem=recv_sem.at[step, 2 * d + slot],
                        device_id={"space": other},
                        device_id_type=MESH,
                    )
                    copies[d, slot].start()

        def z_pass(i, inner):
            def load(p, _):
                return along_lanes(one[back_rows(i * BACKS + p), :], inv_ref[...])

            def update(p, values):
                for n in range(BACK // LANES):
                    pair = (i * BACKS + p) * (BACK // LANES) + n
                    rows = half_rows(pair)
                    re, im = updated(pair, *(values[(2 * n + h) * N : (2 * n + h + 1) * N] for h in range(2)))
                    fre[rows, :] = re
                    fim[rows, :] = im
                    put_drive(
                        pair,
                        pot[rows, :] * re + DAMP * im + source_ref[0, rows, :],
                        pot[rows, :] * im - DAMP * re + source_ref[1, rows, :],
                    )

            staggered(BACKS, (load, update))
            return inner

        lax.fori_loop(0, ROWS // BACK // BACKS, z_pass, 0)

        def difference(d, slot):
            if not remote:
                return -faces[d, 1 - slot]
            copies[d, slot].wait_recv()
            there = (has_below if slot == 0 else has_above)[d]
            return there * recv[step, 2 * d + slot] - faces[d, 1 - slot]

        for d in (0, 1):
            for slot in range(2):
                drive[edges[d][slot], :] = drive[edges[d][slot], :] + difference(d, slot)
        zcor[0] = difference(2, 0)
        upper_end = difference(2, 1)
        zcor[1] = upper_end
        zcor[2] = jnp.where(low, -1.0, 1.0) * turned(upper_end)
        for copy in copies.values():
            copy.wait_send()

    def grad_copy(owner, slot):
        return pltpu.make_async_remote_copy(
            src_ref=gsend.at[owner],
            dst_ref=grecv.at[slot],
            send_sem=gsend_sem.at[owner],
            recv_sem=grecv_sem.at[slot],
            device_id={"src": owner},
            device_id_type=MESH,
        )

    def out_copy(i, part):
        rows = pl.ds(pl.multiple_of(i * (CH // 2), CH // 2), CH // 2)
        return pltpu.make_async_copy(
            packed.at[part, rows], out_hbm.at[part, rows], out_sem.at[i, part]
        )

    def last_pass(k, carry):
        i = lax.rem(me // 2 + 2 + lax.rem(k, 4) - k // 4, 4) * 2 + lax.rem(me + 1 - k // 4, 2)
        items = CH // BACK

        def load(p, _):
            return back_swap(i * items + p, False)

        def update(p, values):
            values = along_lanes(values, inv_ref[...])
            for n in range(BACK // LANES):
                pair = (i * items + p) * (BACK // LANES) + n
                new = updated(pair, *(values[(2 * n + h) * N : (2 * n + h + 1) * N] for h in range(2)))
                fre[half_rows(pair), :] = new[0]
                fim[half_rows(pair), :] = new[1]
                terms = []
                for part in range(2):
                    sides = [adjoint[part, plane_rows(pair, half), :].astype(F32) for half in range(2)]
                    terms.append(jnp.concatenate(sides, axis=1) * new[part])
                to = (p * (BACK // LANES) + n) * N
                gsend[i, to : to + N, :] = terms[0] - terms[1]

        staggered(items, (load, update))
        for part in range(2):
            out_copy(i, part).start()
        if remote:

            @pl.when(k < SRC - 1)
            def _():
                grad_copy(i, me).start()

        return carry

    def finish():
        loads[6].wait()
        lax.fori_loop(0, SRC, last_pass, 0)
        total = gsend[me]
        if remote:
            for k in range(1, SRC):
                other = lax.rem(me + k, SRC)
                grad_copy(other, other).wait_recv()
                total = total + grecv[other]
        for n in range(SLAB // 2):
            for half in range(2):
                to = (2 * n + half) * N
                grad_ref[to : to + N, :] = total[n * N : (n + 1) * N, half * N : (half + 1) * N]
        if remote:
            for k in range(1, SRC):
                grad_copy(lax.rem(me + k, SRC), me).wait_send()
        for i in range(SRC):
            for part in range(2):
                out_copy(i, part).wait()

    def term(step, carry):
        forward()
        middle()
        pl.when(step < TERMS)(lambda: finish_term(step))
        pl.when(step == TERMS)(finish)
        return carry

    lax.fori_loop(0, TERMS + 1, term, 0)


def series(medium, source, adjoint, remote=True):
    k = np.arange(N)
    eig = 2.0 - 2.0 * np.cos(2.0 * np.pi / N * k)
    pair = (eig[:, None] + np.tile(eig, 2)[None, :] - 1.0).astype(np.float32)
    wave = np.stack([np.cos(2.0 * np.pi / N * k), np.sin(2.0 * np.pi / N * k)])
    wave = np.repeat(wave[:, :, None], LANES, axis=2).astype(np.float32)
    half = (ROWS // 2, LANES)
    big = lambda: pltpu.VMEM((ROWS, LANES), F32)
    pitch = lambda: pltpu.VMEM((N * PITCH, LANES), F32)
    square = pltpu.VMEM((2 * LANES, 2 * LANES), BF16)
    planes = lambda *count: pltpu.VMEM(count + (N, LANES), F32)
    vmem, anywhere = pl.BlockSpec(memory_space=pltpu.VMEM), pl.BlockSpec(memory_space=pl.ANY)
    hbm = pl.BlockSpec(memory_space=pltpu.HBM)
    return pl.pallas_call(
        functools.partial(series_kernel, remote),
        out_shape=(
            jax.ShapeDtypeStruct((2,) + half, F32),
            jax.ShapeDtypeStruct((CH, N), F32),
        ),
        in_specs=[pl.BlockSpec(memory_space=pltpu.SMEM)] + [vmem] + [hbm] * 7,
        out_specs=(anywhere, vmem),
        scratch_shapes=[
            pltpu.VMEM((2,) + half, F32),
            big(), pitch(), pitch(), big(), big(),
            pltpu.VMEM(half, F32),
            pltpu.VMEM((ROWS, N), F32),
            planes(), planes(2),
            square, square, square,
            pltpu.VMEM((2, ROWS, N), BF16),
            planes(3, 2), planes(3, 2), planes(), pltpu.VMEM((LANES, LANES), F32),
            planes(3), planes(3), planes(TERMS, 6),
            pltpu.VMEM((SRC, CH // 2, LANES), F32),
            pltpu.VMEM((SRC, CH // 2, LANES), F32),
            pltpu.SemaphoreType.DMA((TERMS, 6)),
            pltpu.SemaphoreType.DMA((TERMS, 6)),
            pltpu.SemaphoreType.DMA((SRC,)),
            pltpu.SemaphoreType.DMA((SRC,)),
            pltpu.SemaphoreType.DMA((SRC, 2)),
            pltpu.SemaphoreType.DMA((7,)),
        ],
        compiler_params=pltpu.CompilerParams(
            collective_id=0 if remote else None,
            has_side_effects=remote,
            vmem_limit_bytes=48 * 1024 * 1024,
        ),
    )(
        jnp.asarray(eig.astype(np.float32)),
        source,
        medium.reshape(ROWS, N),
        jnp.asarray(pair),
        jnp.asarray(wave),
        jnp.asarray(dft_table(-1.0)),
        jnp.asarray(dft_table(1.0)),
        jnp.asarray(dft_table(-1.0).T),
        adjoint.reshape(2, ROWS, N),
    )


def unpack_kernel(in_ref, out_ref):
    for part in range(2):
        for n in range(in_ref.shape[1] // N):
            pair = in_ref[part, n * N : (n + 1) * N, :]
            for half in range(2):
                to = (2 * n + half) * N
                out_ref[part, to : to + N, :] = pair[:, half * N : (half + 1) * N]


def unpack(packed, steps=4):
    rows = ROWS // steps
    return pl.pallas_call(
        unpack_kernel,
        grid=(steps,),
        out_shape=jax.ShapeDtypeStruct((2, ROWS, N), F32),
        in_specs=[pl.BlockSpec((2, rows // 2, LANES), lambda i: (0, i, 0))],
        out_specs=pl.BlockSpec((2, rows, N), lambda i: (0, i, 0)),
        compiler_params=pltpu.CompilerParams(vmem_limit_bytes=12 * 1024 * 1024),
    )(packed)


def local(medium, source_cells, source_weights, adjoint):
    box = lax.axis_index("space").astype(jnp.int32).reshape(1)
    source = place(box, source_cells, source_weights)
    packed, owned = series(medium, source, adjoint)
    return unpack(packed).reshape(2, 1, 1, N, N, N), owned.reshape(1, SLAB, N, N)


def solution(mesh):
    placed = (
        P("space", None, None, None),
        P("src", None),
        P(None, "src", None),
        P(None, "src", "space", None, None, None),
    )
    return jax.shard_map(
        local,
        mesh=mesh,
        in_specs=placed,
        out_specs=(P(None, "src", "space", None, None, None), P("space", "src", None, None)),
        check_vma=False,
    )
```

profile of v0, /device:TPU:1, one launch (start us, length us, event | category | flops | bytes accessed | tf_op | source)
XLA Modules:
  0.0 64.6 jit_solution(12362090350461018488)
XLA Ops:
  0.6 0.0 copy-start
  0.6 0.0 copy-start.1
  0.7 0.0 copy-start.2
  0.7 0.0 copy-start.3
  0.7 0.0 copy-start.4
  0.7 0.8 %copy-done.4 = f32[2,1,4096]{2,1,0:T(1,128)S(1)} copy-done((f32[2,1,4096]{2,1,0:T(1,128)S(1)}, f32[2,1,4096]{2,1,0:T(1,128)}, u32[]{:S(2)}) %copy-start.4) | copy-done | bytes 32792
  1.5 0.0 copy-start.6
  1.5 0.7 %copy-done.6 = s32[1,4096]{1,0:T(1,128)S(1)} copy-done((s32[1,4096]{1,0:T(1,128)S(1)}, s32[1,4096]{1,0:T(1,128)}, u32[]{:S(2)}) %copy-start.6) | copy-done | bytes 16408
  2.2 0.0 copy-start.5
  2.2 0.0 copy-start.7
  2.2 3.2 %shard_map.113.source_ref = f32[2,2048,128]{2,1,0:T(8,128)S(1)} custom-call(s32[1]{0:T(128)} %bitcast.box_ref, s32[32,128]{1,0:T(8,128)S(1)} %bitcast.11, f32[2,32,128]{2,1,0:T(8,128)S(1)} %bitcast.10), custom_call_target="tpu_custom_call" | custom-call | tf_op jit(solution)/shard_map/pallas_call | solution.py:157
  5.5 0.0 copy-done
  5.5 0.0 copy-done.1
  5.5 0.0 copy-done.2
  5.5 0.0 copy-done.3
  5.5 0.0 copy-done.5
  5.5 0.0 copy-done.7
  5.5 55.5 %shard_map.114 = (f32[2,2048,128]{2,1,0:T(8,128)S(1)}, f32[512,64]{1,0:T(8,128)S(1)}) custom-call(f32[64]{0:T(128)S(1)} %copy-done.7, f32[2,2048,128]{2,1,0:T(8,128)S(1)} %shard_map.113.source_ref, f32[4096,64]{1,0:T(8,128)} %bitcast.13, f32[64,128]{1,0:T(8,128)S(1)} %copy-done.5, f32[2,64,128]{2,1,0:T(8,128)S(1)} %copy-done.3, ...), custom_call_target="tpu_custom_call" | custom-call | tf_op jit(solution)/shard_map/pallas_call | solution.py:519
  61.1 2.8 %shard_map.115 = f32[2,4096,64]{2,1,0:T(8,128)} custom-call(f32[2,2048,128]{2,1,0:T(8,128)S(1)} %get-tuple-element.4.in_ref), custom_call_target="tpu_custom_call" | custom-call | tf_op jit(solution)/shard_map/pallas_call | solution.py:575
  63.9 0.7 %copy.14 = f32[1,8,64,64]{3,2,1,0:T(8,128)} copy(f32[1,8,64,64]{3,2,1,0:T(8,128)S(1)} %bitcast.9) | data formatting | bytes 262144
Async XLA Ops:
  0.6 4.8 %copy-start = (bf16[256,256]{1,0:T(8,128)(2,1)S(1)}, bf16[256,256]{1,0:T(8,128)(2,1)}, u32[]{:S(2)}) copy-start(bf16[256,256]{1,0:T(8,128)(2,1)} %constant.23.clone.turn_hbm) | copy-start | bytes 393220
  0.6 4.8 %copy-start.1 = (bf16[256,256]{1,0:T(8,128)(2,1)S(1)}, bf16[256,256]{1,0:T(8,128)(2,1)}, u32[]{:S(2)}) copy-start(bf16[256,256]{1,0:T(8,128)(2,1)} %constant.22.clone.inv_hbm) | copy-start | bytes 393220
  0.7 4.8 %copy-start.2 = (bf16[256,256]{1,0:T(8,128)(2,1)S(1)}, bf16[256,256]{1,0:T(8,128)(2,1)}, u32[]{:S(2)}) copy-start(bf16[256,256]{1,0:T(8,128)(2,1)} %constant.21.clone.fwd_hbm) | copy-start | bytes 393220
  0.7 4.8 %copy-start.3 = (f32[2,64,128]{2,1,0:T(8,128)S(1)}, f32[2,64,128]{2,1,0:T(8,128)}, u32[]{:S(2)}) copy-start(f32[2,64,128]{2,1,0:T(8,128)} %constant.20.clone.wave_hbm) | copy-start | bytes 196612
  0.7 0.8 %copy-start.4 = (f32[2,1,4096]{2,1,0:T(1,128)S(1)}, f32[2,1,4096]{2,1,0:T(1,128)}, u32[]{:S(2)}) copy-start(f32[2,1,4096]{2,1,0:T(1,128)} %param.12) | copy-start | bytes 98308
  1.5 0.7 %copy-start.6 = (s32[1,4096]{1,0:T(1,128)S(1)}, s32[1,4096]{1,0:T(1,128)}, u32[]{:S(2)}) copy-start(s32[1,4096]{1,0:T(1,128)} %param.11) | copy-start | bytes 49156
  2.2 3.3 %copy-start.5 = (f32[64,128]{1,0:T(8,128)S(1)}, f32[64,128]{1,0:T(8,128)}, u32[]{:S(2)}) copy-start(f32[64,128]{1,0:T(8,128)} %constant.19.clone.pair_hbm) | copy-start | bytes 98308
  2.2 3.3 %copy-start.7 = (f32[64]{0:T(128)S(1)}, f32[64]{0:T(128)}, u32[]{:S(2)}) copy-start(f32[64]{0:T(128)} %constant.18.clone.eig_ref) | copy-start | bytes 772
where the time goes:
time: 64.8 us; the launch traced here: 64.6 us
  Pallas kernels  61.6 us (95%)
  local copies, waits for them, and re-layouts  2.28 us (4%)
  between operations  0.74 us (1%)
    pallas_call x1, Pallas kernels, series(): pl.pallas_call(functools.partial(series_kernel, remote), out_shape=(jax.S...  55.5 us
    pallas_call x1, Pallas kernels, place(): pl.pallas_call(place_kernel, out_shape=jax.ShapeDtypeStruct((2, ROWS // 2...  3.22 us
    pallas_call x1, Pallas kernels, unpack(): pl.pallas_call(unpack_kernel, grid=(steps,), out_shape=jax.ShapeDtypeStru...  2.84 us
    unnamed x17, local copies, waits for them, and re-layouts  2.28 us

commit v1 on v0

--- a/solution.py
+++ b/solution.py
@@ -219,15 +219,17 @@
     low = lower_half(N)
 
     def table(z, carry):
-        rows = pl.ds(pl.multiple_of(z * N, N), N)
         shifted = pair_ref[...] + eig_ref[z]
         scale = 1.0 / ((shifted * shifted + DAMP * DAMP) * float(N**3))
-        kre[rows, :] = shifted * scale
-        kim[rows, :] = jnp.where(low, -DAMP, DAMP) * scale
+        real, imag = shifted * scale, jnp.where(low, -DAMP, DAMP) * scale
+        for same in (z, lax.rem(N - z, N)):
+            rows = pl.ds(pl.multiple_of(same * N, N), N)
+            kre[rows, :] = real
+            kim[rows, :] = imag
         return carry
 
     loads[0].wait()
-    lax.fori_loop(0, N, table, 0)
+    lax.fori_loop(0, N // 2 + 1, table, 0)
 
     def half_rows(pair):
         return pl.ds(pl.multiple_of(pair * N, N), N)
@@ -482,10 +484,7 @@
                 other = lax.rem(me + k, SRC)
                 grad_copy(other, other).wait_recv()
                 total = total + grecv[other]
-        for n in range(SLAB // 2):
-            for half in range(2):
-                to = (2 * n + half) * N
-                grad_ref[to : to + N, :] = total[n * N : (n + 1) * N, half * N : (half + 1) * N]
+        grad_ref[...] = total
         if remote:
             for k in range(1, SRC):
                 grad_copy(lax.rem(me + k, SRC), me).wait_send()
@@ -520,7 +519,7 @@
         functools.partial(series_kernel, remote),
         out_shape=(
             jax.ShapeDtypeStruct((2,) + half, F32),
-            jax.ShapeDtypeStruct((CH, N), F32),
+            jax.ShapeDtypeStruct((CH // 2, LANES), F32),
         ),
         in_specs=[pl.BlockSpec(memory_space=pltpu.SMEM)] + [vmem] + [hbm] * 7,
         out_specs=(anywhere, vmem),
@@ -561,32 +560,38 @@
     )
 
 
-def unpack_kernel(in_ref, out_ref):
-    for part in range(2):
-        for n in range(in_ref.shape[1] // N):
-            pair = in_ref[part, n * N : (n + 1) * N, :]
+def unpack_kernel(in_ref, total_ref, out_ref, grad_ref):
+    for source, target in ((in_ref.at[0], out_ref.at[0]), (in_ref.at[1], out_ref.at[1]), (total_ref, grad_ref)):
+        for n in range(source.shape[0] // N):
+            pair = source[n * N : (n + 1) * N, :]
             for half in range(2):
                 to = (2 * n + half) * N
-                out_ref[part, to : to + N, :] = pair[:, half * N : (half + 1) * N]
-
-
-def unpack(packed, steps=4):
-    rows = ROWS // steps
+                target[to : to + N, :] = pair[:, half * N : (half + 1) * N]
+
+
+def unpack(packed, total, steps=4):
+    rows, own = ROWS // steps, CH // steps
     return pl.pallas_call(
         unpack_kernel,
         grid=(steps,),
-        out_shape=jax.ShapeDtypeStruct((2, ROWS, N), F32),
-        in_specs=[pl.BlockSpec((2, rows // 2, LANES), lambda i: (0, i, 0))],
-        out_specs=pl.BlockSpec((2, rows, N), lambda i: (0, i, 0)),
+        out_shape=(jax.ShapeDtypeStruct((2, ROWS, N), F32), jax.ShapeDtypeStruct((CH, N), F32)),
+        in_specs=[
+            pl.BlockSpec((2, rows // 2, LANES), lambda i: (0, i, 0)),
+            pl.BlockSpec((own // 2, LANES), lambda i: (i, 0)),
+        ],
+        out_specs=(
+            pl.BlockSpec((2, rows, N), lambda i: (0, i, 0)),
+            pl.BlockSpec((own, N), lambda i: (i, 0)),
+        ),
         compiler_params=pltpu.CompilerParams(vmem_limit_bytes=12 * 1024 * 1024),
-    )(packed)
+    )(packed, total)
 
 
 def local(medium, source_cells, source_weights, adjoint):
     box = lax.axis_index("space").astype(jnp.int32).reshape(1)
     source = place(box, source_cells, source_weights)
-    packed, owned = series(medium, source, adjoint)
-    return unpack(packed).reshape(2, 1, 1, N, N, N), owned.reshape(1, SLAB, N, N)
+    field, owned = unpack(*series(medium, source, adjoint))
+    return field.reshape(2, 1, 1, N, N, N), owned.reshape(1, SLAB, N, N)
 
 
 def solution(mesh):

time: 64.8 us -> 63.6 us (0.981)
  local copies, waits for them, and re-layouts: 2.28 us -> 1.57 us
    unnamed x17 -> x16, local copies, waits for them, and re-layouts: 2.28 us -> 1.57 us
where the time goes in v1:
time: 63.6 us; the launch traced here: 63.4 us
  Pallas kernels  61.1 us (96%)
  local copies, waits for them, and re-layouts  1.57 us (2%)
  between operations  0.74 us (1%)
    pallas_call x1, Pallas kernels, series(): pl.pallas_call(functools.partial(series_kernel, remote), out_shape=(jax.S...  55 us
    pallas_call x1, Pallas kernels, place(): pl.pallas_call(place_kernel, out_shape=jax.ShapeDtypeStruct((2, ROWS // 2...  3.22 us
    pallas_call x1, Pallas kernels, unpack(): pl.pallas_call(unpack_kernel, grid=(steps,), out_shape=(jax.ShapeDtypeStr...  2.89 us
    unnamed x16, local copies, waits for them, and re-layouts  1.57 us

profile of v1, /device:TPU:1, one launch (start us, length us, event | category | flops | bytes accessed | tf_op | source)
XLA Modules:
  0.0 63.4 jit_solution(6762742563085175433)
XLA Ops:
  0.6 0.0 copy-start
  0.6 0.0 copy-start.1
  0.7 0.0 copy-start.2
  0.7 0.0 copy-start.3
  0.7 0.0 copy-start.4
  0.7 0.8 %copy-done.4 = f32[2,1,4096]{2,1,0:T(1,128)S(1)} copy-done((f32[2,1,4096]{2,1,0:T(1,128)S(1)}, f32[2,1,4096]{2,1,0:T(1,128)}, u32[]{:S(2)}) %copy-start.4) | copy-done | bytes 32792
  1.5 0.0 copy-start.6
  1.5 0.7 %copy-done.6 = s32[1,4096]{1,0:T(1,128)S(1)} copy-done((s32[1,4096]{1,0:T(1,128)S(1)}, s32[1,4096]{1,0:T(1,128)}, u32[]{:S(2)}) %copy-start.6) | copy-done | bytes 16408
  2.2 0.0 copy-start.5
  2.2 0.0 copy-start.7
  2.2 3.2 %shard_map.113.source_ref = f32[2,2048,128]{2,1,0:T(8,128)S(1)} custom-call(s32[1]{0:T(128)} %bitcast.box_ref, s32[32,128]{1,0:T(8,128)S(1)} %bitcast.10, f32[2,32,128]{2,1,0:T(8,128)S(1)} %bitcast.9), custom_call_target="tpu_custom_call" | custom-call | tf_op jit(solution)/shard_map/pallas_call | solution.py:157
  5.5 0.0 copy-done
  5.5 0.0 copy-done.1
  5.5 0.0 copy-done.2
  5.5 0.0 copy-done.3
  5.5 0.0 copy-done.5
  5.5 0.0 copy-done.7
  5.5 55.0 %shard_map.114 = (f32[2,2048,128]{2,1,0:T(8,128)S(1)}, f32[256,128]{1,0:T(8,128)S(1)}) custom-call(f32[64]{0:T(128)S(1)} %copy-done.7, f32[2,2048,128]{2,1,0:T(8,128)S(1)} %shard_map.113.source_ref, f32[4096,64]{1,0:T(8,128)} %bitcast.11, f32[64,128]{1,0:T(8,128)S(1)} %copy-done.5, f32[2,64,128]{2,1,0:T(8,128)S(1)} %copy-done.3, ...), custom_call_target="tpu_custom_call" | custom-call | tf_op jit(solution)/shard_map/pallas_call | solution.py:518
  60.6 2.9 %shard_map.115 = (f32[2,4096,64]{2,1,0:T(8,128)}, f32[512,64]{1,0:T(8,128)}) custom-call(f32[2,2048,128]{2,1,0:T(8,128)S(1)} %get-tuple-element.6.in_ref, f32[256,128]{1,0:T(8,128)S(1)} %get-tuple-element.7.total_ref), custom_call_target="tpu_custom_call" | custom-call | tf_op jit(solution)/shard_map/pallas_call | solution.py:574
Async XLA Ops:
  0.6 4.8 %copy-start = (bf16[256,256]{1,0:T(8,128)(2,1)S(1)}, bf16[256,256]{1,0:T(8,128)(2,1)}, u32[]{:S(2)}) copy-start(bf16[256,256]{1,0:T(8,128)(2,1)} %constant.23.clone.turn_hbm) | copy-start | bytes 393220
  0.6 4.8 %copy-start.1 = (bf16[256,256]{1,0:T(8,128)(2,1)S(1)}, bf16[256,256]{1,0:T(8,128)(2,1)}, u32[]{:S(2)}) copy-start(bf16[256,256]{1,0:T(8,128)(2,1)} %constant.22.clone.inv_hbm) | copy-start | bytes 393220
  0.7 4.8 %copy-start.2 = (bf16[256,256]{1,0:T(8,128)(2,1)S(1)}, bf16[256,256]{1,0:T(8,128)(2,1)}, u32[]{:S(2)}) copy-start(bf16[256,256]{1,0:T(8,128)(2,1)} %constant.21.clone.fwd_hbm) | copy-start | bytes 393220
  0.7 4.8 %copy-start.3 = (f32[2,64,128]{2,1,0:T(8,128)S(1)}, f32[2,64,128]{2,1,0:T(8,128)}, u32[]{:S(2)}) copy-start(f32[2,64,128]{2,1,0:T(8,128)} %constant.20.clone.wave_hbm) | copy-start | bytes 196612
  0.7 0.8 %copy-start.4 = (f32[2,1,4096]{2,1,0:T(1,128)S(1)}, f32[2,1,4096]{2,1,0:T(1,128)}, u32[]{:S(2)}) copy-start(f32[2,1,4096]{2,1,0:T(1,128)} %param.12) | copy-start | bytes 98308
  1.5 0.7 %copy-start.6 = (s32[1,4096]{1,0:T(1,128)S(1)}, s32[1,4096]{1,0:T(1,128)}, u32[]{:S(2)}) copy-start(s32[1,4096]{1,0:T(1,128)} %param.11) | copy-start | bytes 49156
  2.2 3.3 %copy-start.5 = (f32[64,128]{1,0:T(8,128)S(1)}, f32[64,128]{1,0:T(8,128)}, u32[]{:S(2)}) copy-start(f32[64,128]{1,0:T(8,128)} %constant.19.clone.pair_hbm) | copy-start | bytes 98308
  2.2 3.3 %copy-start.7 = (f32[64]{0:T(128)S(1)}, f32[64]{0:T(128)}, u32[]{:S(2)}) copy-start(f32[64]{0:T(128)} %constant.18.clone.eig_ref) | copy-start | bytes 772

commit v2 on v1

--- a/solution.py
+++ b/solution.py
@@ -17,7 +17,7 @@
 SLAB = N // SRC
 CH = SLAB * N
 DAMP = 0.25
-PITCH = 72
+PITCH = 68
 BACK, BACKS = 512, 4
 ITEM = 2048
 MESH = pl.DeviceIdType.MESH
@@ -238,7 +238,7 @@
         return pl.ds(pl.multiple_of((2 * pair + half) * N, N), N)
 
     def pitched(pair, half):
-        return pl.ds(pl.multiple_of((2 * pair + half) * PITCH, 8), N)
+        return pl.ds((2 * pair + half) * PITCH, N)
 
     def put_drive(pair, re, im):
         for half, rows in enumerate(trade(re, im)):
@@ -325,7 +325,7 @@
         planes = []
         for n in range(BACK // N):
             x = item * (BACK // N) + n
-            plane = two[pl.ds(pl.multiple_of(x * PITCH, 8), N), :]
+            plane = two[pl.ds(x * PITCH, N), :]
             planes.append(plane)
             if ends:
                 sums[0, pl.ds(x, 1), :] = jnp.sum(plane, axis=0, keepdims=True)

time: 63.6 us -> 63.1 us (level)
  no operation moved by 1% of the time
where the time goes in v2:
time: 63.1 us; the launch traced here: 63 us
  Pallas kernels  60.6 us (96%)
  local copies, waits for them, and re-layouts  1.57 us (2%)
  between operations  0.74 us (1%)
    pallas_call x1, Pallas kernels, series(): pl.pallas_call(functools.partial(series_kernel, remote), out_shape=(jax.S...  54.5 us
    pallas_call x1, Pallas kernels, place(): pl.pallas_call(place_kernel, out_shape=jax.ShapeDtypeStruct((2, ROWS // 2...  3.22 us
    pallas_call x1, Pallas kernels, unpack(): pl.pallas_call(unpack_kernel, grid=(steps,), out_shape=(jax.ShapeDtypeStr...  2.89 us
    unnamed x16, local copies, waits for them, and re-layouts  1.57 us

profile of v2, /device:TPU:1, one launch (start us, length us, event | category | flops | bytes accessed | tf_op | source)
XLA Modules:
  0.0 63.0 jit_solution(14840686118883980395)
XLA Ops:
  0.6 0.0 copy-start
  0.6 0.0 copy-start.1
  0.7 0.0 copy-start.2
  0.7 0.0 copy-start.3
  0.7 0.0 copy-start.4
  0.7 0.8 %copy-done.4 = f32[2,1,4096]{2,1,0:T(1,128)S(1)} copy-done((f32[2,1,4096]{2,1,0:T(1,128)S(1)}, f32[2,1,4096]{2,1,0:T(1,128)}, u32[]{:S(2)}) %copy-start.4) | copy-done | bytes 32792
  1.5 0.0 copy-start.6
  1.5 0.7 %copy-done.6 = s32[1,4096]{1,0:T(1,128)S(1)} copy-done((s32[1,4096]{1,0:T(1,128)S(1)}, s32[1,4096]{1,0:T(1,128)}, u32[]{:S(2)}) %copy-start.6) | copy-done | bytes 16408
  2.2 0.0 copy-start.5
  2.2 0.0 copy-start.7
  2.2 3.2 %shard_map.113.source_ref = f32[2,2048,128]{2,1,0:T(8,128)S(1)} custom-call(s32[1]{0:T(128)} %bitcast.box_ref, s32[32,128]{1,0:T(8,128)S(1)} %bitcast.10, f32[2,32,128]{2,1,0:T(8,128)S(1)} %bitcast.9), custom_call_target="tpu_custom_call" | custom-call | tf_op jit(solution)/shard_map/pallas_call | solution.py:157
  5.5 0.0 copy-done
  5.5 0.0 copy-done.1
  5.5 0.0 copy-done.2
  5.5 0.0 copy-done.3
  5.5 0.0 copy-done.5
  5.5 0.0 copy-done.7
  5.5 54.5 %shard_map.114 = (f32[2,2048,128]{2,1,0:T(8,128)S(1)}, f32[256,128]{1,0:T(8,128)S(1)}) custom-call(f32[64]{0:T(128)S(1)} %copy-done.7, f32[2,2048,128]{2,1,0:T(8,128)S(1)} %shard_map.113.source_ref, f32[4096,64]{1,0:T(8,128)} %bitcast.11, f32[64,128]{1,0:T(8,128)S(1)} %copy-done.5, f32[2,64,128]{2,1,0:T(8,128)S(1)} %copy-done.3, ...), custom_call_target="tpu_custom_call" | custom-call | tf_op jit(solution)/shard_map/pallas_call | solution.py:518
  60.1 2.9 %shard_map.115 = (f32[2,4096,64]{2,1,0:T(8,128)}, f32[512,64]{1,0:T(8,128)}) custom-call(f32[2,2048,128]{2,1,0:T(8,128)S(1)} %get-tuple-element.6.in_ref, f32[256,128]{1,0:T(8,128)S(1)} %get-tuple-element.7.total_ref), custom_call_target="tpu_custom_call" | custom-call | tf_op jit(solution)/shard_map/pallas_call | solution.py:574
Async XLA Ops:
  0.6 4.8 %copy-start = (bf16[256,256]{1,0:T(8,128)(2,1)S(1)}, bf16[256,256]{1,0:T(8,128)(2,1)}, u32[]{:S(2)}) copy-start(bf16[256,256]{1,0:T(8,128)(2,1)} %constant.23.clone.turn_hbm) | copy-start | bytes 393220
  0.6 4.8 %copy-start.1 = (bf16[256,256]{1,0:T(8,128)(2,1)S(1)}, bf16[256,256]{1,0:T(8,128)(2,1)}, u32[]{:S(2)}) copy-start(bf16[256,256]{1,0:T(8,128)(2,1)} %constant.22.clone.inv_hbm) | copy-start | bytes 393220
  0.7 4.8 %copy-start.2 = (bf16[256,256]{1,0:T(8,128)(2,1)S(1)}, bf16[256,256]{1,0:T(8,128)(2,1)}, u32[]{:S(2)}) copy-start(bf16[256,256]{1,0:T(8,128)(2,1)} %constant.21.clone.fwd_hbm) | copy-start | bytes 393220
  0.7 4.8 %copy-start.3 = (f32[2,64,128]{2,1,0:T(8,128)S(1)}, f32[2,64,128]{2,1,0:T(8,128)}, u32[]{:S(2)}) copy-start(f32[2,64,128]{2,1,0:T(8,128)} %constant.20.clone.wave_hbm) | copy-start | bytes 196612
  0.7 0.8 %copy-start.4 = (f32[2,1,4096]{2,1,0:T(1,128)S(1)}, f32[2,1,4096]{2,1,0:T(1,128)}, u32[]{:S(2)}) copy-start(f32[2,1,4096]{2,1,0:T(1,128)} %param.12) | copy-start | bytes 98308
  1.5 0.7 %copy-start.6 = (s32[1,4096]{1,0:T(1,128)S(1)}, s32[1,4096]{1,0:T(1,128)}, u32[]{:S(2)}) copy-start(s32[1,4096]{1,0:T(1,128)} %param.11) | copy-start | bytes 49156
  2.2 3.3 %copy-start.5 = (f32[64,128]{1,0:T(8,128)S(1)}, f32[64,128]{1,0:T(8,128)}, u32[]{:S(2)}) copy-start(f32[64,128]{1,0:T(8,128)} %constant.19.clone.pair_hbm) | copy-start | bytes 98308
  2.2 3.3 %copy-start.7 = (f32[64]{0:T(128)S(1)}, f32[64]{0:T(128)}, u32[]{:S(2)}) copy-start(f32[64]{0:T(128)} %constant.18.clone.eig_ref) | copy-start | bytes 772
